TPU v7x, 128 devices: a whole 4x4x4 slice. The times are simulated.
128 devices in a mesh: ctx: 16 (over x_lo, z, core), mp: 4 (over y), rep: 2 (over x_hi).
Axes of the slice: x: 4 (x_hi: 2, x_lo: 2; x = x_hi * 2 + x_lo), y: 4, z: 4, core: 2. Of those that a mesh axis runs over, the one named last changes fastest.
Arguments:
- token_pages: bfloat16 [128, 128, 2048], P('ctx'), may hold values from -13 to 13
- page_table: int32 [128], P('ctx'), may hold values from 0 to 7, as said below
- live_flags: int32 [128], P('ctx'), may hold values from 0 to 1, as said below
- lengths: int32 [32], replicated, may hold values from 1 to 1024, as said below
- decay_floor: float32 [2048], P(('mp', 'rep')), may hold values from 0.85 to 0.9998
- mixer_gain: float32 [2048], replicated, may hold values from 0.5 to 1.5
- feed_gain: float32 [2048], replicated, may hold values from 0.5 to 1.5
- trainer_mixer_in: float32 [3, 2048, 2048], P(None, ('ctx', 'mp')), may hold values from -0.125 to 0.125
- trainer_mixer_out: float32 [2048, 2048], P(None, ('ctx', 'mp')), may hold values from -0.125 to 0.125
- trainer_gate_up: float32 [2, 2048, 5632], P(None, ('ctx', 'mp')), may hold values from -0.125 to 0.125
- trainer_down: float32 [5632, 2048], P(None, ('ctx', 'mp')), may hold values from -0.078125 to 0.078125
Outputs:
- layer_output: bfloat16 [16384, 2048], P(('ctx', 'rep'), 'mp')
Inputs may be any that keep to these rules, and one draw needn't show every extreme that they name: `page_table`: within each device's block of 8 entries every value 0 to 7 appears once. `live_flags`: in each device's block of 8 flags at least half (rounded down, and never fewer than one) are ones, and some device's block is all ones. The lengths sum to 128 times the number of ones in live_flags; one prompt has exactly 1024 tokens.
All inputs are finite; a program needn't handle non-finite values.
Results may differ from a plain program's by a relative error of at most 0.015.
Values may be sent and summed in bfloat16 or wider, within the bound.
A program may use at most 192 MiB of HBM per device.

v0:
```python
import jax
import jax.numpy as jnp
from jax import lax
from jax.sharding import PartitionSpec as P

D = 2048
HEADS = 16
norm_eps = 1e-05


def prefix(value, axis, join, neutral):
    count, mine = (lax.axis_size(axis), lax.axis_index(axis))
    pieces = lax.all_gather(value, axis)
    total = jnp.full_like(value, 0) + jnp.asarray(neutral, value.dtype)

    def prefix_step(position, total):
        longer = join(total, pieces[position])
        return jnp.where(position < mine, longer, total)

    return lax.fori_loop(0, count - 1, prefix_step, total)


def entering_2(shard, axis, combine, identity):
    peers, position = (lax.axis_size(axis), lax.axis_index(axis))
    everything = jax.tree.map(
        lambda part, kind: lax.all_gather(part.astype(kind), axis),
        shard,
        (jnp.bfloat16, jnp.bfloat16),
    )
    start = jax.tree.map(
        lambda part, zero: jnp.broadcast_to(jnp.asarray(zero, part.dtype), part.shape),
        shard,
        identity,
    )

    def entering_step(k, before):
        reached = k < position
        new = combine(
            before, jax.tree.map(lambda part, own: part[k].astype(own.dtype), everything, shard)
        )
        return jax.tree.map(lambda a, b: jnp.where(reached, a, b), new, before)

    return lax.fori_loop(0, peers, entering_step, start)


def rms_scale(values_in, gain):
    mean_sq = jnp.mean(values_in * values_in, axis=-1, keepdims=True)
    return values_in * lax.rsqrt(mean_sq + norm_eps) * gain


def block_recurrence(queries, keys_in, values_in, log_decay, reset_count, state_init, count_init):
    highest = lax.Precision.HIGHEST

    def advance(carried_in, block_data):
        state, count_before = carried_in
        q_block, k_block, v_block, decay_block, count_block = block_data
        cumulative = jnp.cumsum(decay_block, axis=0)
        q_scaled = q_block * jnp.exp(cumulative)
        k_scaled = k_block * jnp.exp(-cumulative)
        scores = jnp.einsum("thd,shd->hts", q_scaled, k_scaled, precision=highest)
        positions = jnp.arange(count_block.shape[0])
        allowed = (positions[:, None] >= positions[None, :]) & (
            count_block[:, None] == count_block[None, :]
        )
        scores = jnp.where(allowed[None], scores, 0.0)
        outputs = jnp.einsum("hts,shd->thd", scores, v_block, precision=highest)
        from_state = jnp.einsum("thd,hde->the", q_scaled, state, precision=highest)
        outputs = outputs + jnp.where((count_block == count_before)[:, None, None], from_state, 0.0)
        last_count = count_block[-1]
        final_cum = cumulative[-1]
        weight_keys = (
            k_block
            * jnp.exp(final_cum[None] - cumulative)
            * (count_block == last_count).astype(k_block.dtype)[:, None, None]
        )
        retained = jnp.where(
            last_count == count_before, jnp.exp(final_cum)[:, :, None] * state, 0.0
        )
        state_next = retained + jnp.einsum("thd,the->hde", weight_keys, v_block, precision=highest)
        return ((state_next, last_count), outputs)

    final_carry, outputs_all = lax.scan(
        advance, (state_init, count_init), (queries, keys_in, values_in, log_decay, reset_count)
    )
    return (outputs_all, final_carry[0])


def compose_states(earlier, later):
    return (earlier[0] * later[0], later[0][:, :, None] * earlier[1] + later[1])


def add_counts(earlier, later):
    return earlier + later


def shards(
    token_pages,
    page_table,
    live_flags,
    lengths,
    decay_floor,
    mixer_gain,
    feed_gain,
    trainer_mixer_in,
    trainer_mixer_out,
    trainer_gate_up,
    trainer_down,
):
    mp_count = lax.axis_size("mp")
    rep_count = lax.axis_size("rep")
    mp_index = lax.axis_index("mp")
    rep_index = lax.axis_index("rep")
    width_local = trainer_mixer_in.shape[1]
    model_width = trainer_mixer_in.shape[2]
    head_cols = decay_floor.shape[0]
    head_dim = D // HEADS
    local_heads = head_cols // head_dim
    hidden_block = trainer_gate_up.shape[2] // mp_count
    mixer_in = lax.dynamic_index_in_dim(
        trainer_mixer_in.reshape(3, width_local, mp_count, rep_count, head_cols),
        rep_index,
        3,
        keepdims=False,
    )
    mixer_in = jnp.transpose(mixer_in, (1, 2, 0, 3)).reshape(width_local, mp_count, 3 * head_cols)
    mixer_out = lax.dynamic_index_in_dim(
        trainer_mixer_out.reshape(mp_count, rep_count, head_cols, width_local),
        rep_index,
        1,
        keepdims=False,
    )
    mixer_out = jnp.transpose(mixer_out, (2, 0, 1))
    gate_up = trainer_gate_up.reshape(2, width_local, mp_count, hidden_block)
    down_rows = trainer_down.reshape(mp_count, hidden_block, width_local)
    gate_up = jnp.transpose(gate_up, (1, 2, 0, 3)).reshape(width_local, mp_count, 2 * hidden_block)
    down_rows = jnp.transpose(down_rows, (2, 0, 1))
    packed = jnp.concatenate([mixer_in, mixer_out, gate_up, down_rows], axis=2).astype(jnp.bfloat16)
    arrived = lax.all_to_all(packed, "mp", split_axis=1, concat_axis=0, tiled=True)
    arrived = arrived.reshape(mp_count * width_local, packed.shape[2])
    served = lax.all_gather(arrived, "ctx", axis=0, tiled=True)
    w_mixer = served[:, : 3 * head_cols]
    w_output_t = served[:, 3 * head_cols : 4 * head_cols]
    feed_weights = served[:, 4 * head_cols :].reshape(model_width, 3, hidden_block)
    pages_local = token_pages.shape[0]
    page_len = token_pages.shape[1]
    tok_count = pages_local * page_len
    ordered = jnp.take(token_pages, page_table, axis=0).reshape(tok_count, model_width)
    live_tokens = jnp.repeat(live_flags, page_len)
    page_live = live_flags * page_len
    live_total = jnp.sum(page_live)
    stream_base = prefix(live_total, "ctx", add_counts, jnp.zeros((), jnp.int32))
    page_start = stream_base + jnp.cumsum(page_live) - page_live
    positions = (page_start[:, None] + jnp.arange(page_len, dtype=jnp.int32)[None, :]).reshape(
        tok_count
    )
    starts = jnp.cumsum(lengths) - lengths
    resets = (live_tokens == 1) & jnp.any(positions[:, None] == starts[None, :], axis=1)
    reset_count = jnp.cumsum(resets.astype(jnp.int32))
    live_float = live_tokens.astype(jnp.float32)[:, None]
    normed = rms_scale(ordered.astype(jnp.float32), mixer_gain).astype(jnp.bfloat16)
    projected = jnp.dot(normed, w_mixer, preferred_element_type=jnp.float32).reshape(
        tok_count, 3, head_cols
    )
    queries = jax.nn.silu(projected[:, 0])
    forget = decay_floor + (1.0 - decay_floor) * jax.nn.sigmoid(projected[:, 1])
    log_decay = jnp.log(forget) * live_float
    keys_in = (1.0 - forget) * live_float
    values_in = projected[:, 2]
    shape_blocks = (pages_local, page_len, local_heads, head_dim)
    local_out, local_state = block_recurrence(
        queries.reshape(shape_blocks),
        keys_in.reshape(shape_blocks),
        values_in.reshape(shape_blocks),
        log_decay.reshape(shape_blocks),
        reset_count.reshape(pages_local, page_len),
        jnp.zeros((local_heads, head_dim, head_dim), jnp.float32),
        jnp.zeros((), jnp.int32),
    )
    device_decay = jnp.where(
        reset_count[-1] == 0, jnp.exp(jnp.sum(log_decay, axis=0)), 0.0
    ).reshape(local_heads, head_dim)
    identity = (
        jnp.ones((local_heads, head_dim), jnp.float32),
        jnp.zeros((local_heads, head_dim, head_dim), jnp.float32),
    )
    entering = entering_2((device_decay, local_state), "ctx", compose_states, identity)[1]
    cum_device = jnp.cumsum(log_decay, axis=0).reshape(tok_count, local_heads, head_dim)
    scaled_queries = queries.reshape(tok_count, local_heads, head_dim) * jnp.exp(cum_device)
    correction = jnp.einsum(
        "thd,hde->the", scaled_queries, entering, precision=lax.Precision.HIGHEST
    )
    mixed = local_out.reshape(tok_count, local_heads, head_dim) + jnp.where(
        (reset_count == 0)[:, None, None], correction, 0.0
    )
    head_normed = (
        (mixed * lax.rsqrt(jnp.mean(mixed * mixed, axis=-1, keepdims=True) + norm_eps))
        .reshape(tok_count, head_cols)
        .astype(jnp.bfloat16)
    )
    half_rows = tok_count // rep_count
    col_block = model_width // mp_count
    attn_term = lax.dot_general(
        head_normed, w_output_t, (((1,), (1,)), ((), ())), preferred_element_type=jnp.float32
    )
    attn_all = lax.psum(attn_term.astype(jnp.bfloat16), ("mp", "rep")).astype(jnp.float32)
    residual = lax.dynamic_slice_in_dim(ordered, rep_index * half_rows, half_rows, 0).astype(
        jnp.float32
    ) + lax.dynamic_slice_in_dim(attn_all, rep_index * half_rows, half_rows, 0)
    feed_in = rms_scale(residual, feed_gain).astype(jnp.bfloat16)
    gated = jnp.einsum(
        "td,dcf->tcf", feed_in, feed_weights[:, :2], preferred_element_type=jnp.float32
    )
    hidden = (jax.nn.silu(gated[:, 0]) * gated[:, 1]).astype(jnp.bfloat16)
    down_term = lax.dot_general(
        hidden, feed_weights[:, 2], (((1,), (1,)), ((), ())), preferred_element_type=jnp.float32
    )
    summed = lax.psum_scatter(
        down_term.astype(jnp.bfloat16), "mp", scatter_dimension=1, tiled=True
    ).astype(jnp.float32)
    summed = summed + lax.dynamic_slice_in_dim(residual, mp_index * col_block, col_block, 1)
    live_half = lax.dynamic_slice_in_dim(live_tokens, rep_index * half_rows, half_rows, 0)
    return jnp.where(live_half[:, None] == 1, summed, 0.0).astype(jnp.bfloat16)


def solution(mesh):
    in_specs = (
        P("ctx", None, None),
        P("ctx"),
        P("ctx"),
        P(),
        P(("mp", "rep")),
        P(),
        P(),
        P(None, ("ctx", "mp"), None),
        P(None, ("ctx", "mp")),
        P(None, ("ctx", "mp"), None),
        P(None, ("ctx", "mp")),
    )
    out_specs = P(("ctx", "rep"), "mp")
    return jax.shard_map(shards, mesh=mesh, in_specs=in_specs, out_specs=out_specs, check_vma=False)
```

profile of v0, /device:TPU:1, one launch (start us, length us, event | category | flops | bytes accessed | tf_op | source)
XLA Modules:
  0.0 575.1 jit_solution(12584117254873081062)
XLA Ops:
  12.5 22.0 %all_to_all.15 = bf16[32,4,5248]{2,0,1:T(8,128)(2,1)} all-to-all(bf16[32,4,5248]{2,0,1:T(8,128)(2,1)S(1)} %pad_maximum_fusion), channel_id=1, replica_groups=mesh['ctx'=16,'mp'=4,'rep'=2] {'mp'}, dimensions={1} | all-to-all | bytes 2686976 | tf_op jit(solution)/shard_map/all_to_all | solution.py:138
  37.6 13.0 %all-reduce = s32[16]{0:T(128)S(1)} all-reduce(s32[16]{0:T(128)S(1)} %dynamic-update-slice), channel_id=1, replica_groups=mesh['ctx'=16,'mp'=4,'rep'=2] {'ctx'}, use_global_device_ids=true, to_apply=%add | all-reduce | flops 16 | bytes 128
  50.7 18.5 %while.42 = (s32[]{:T(128)}, s32[]{:T(128)}, s32[]{:T(128)}, s32[16]{0:T(128)S(1)}, s32[]{:T(128)}) while((s32[]{:T(128)}, s32[]{:T(128)}, s32[]{:T(128)}, s32[16]{0:T(128)S(1)}, s32[]{:T(128)}) %tuple.96), condition=%wide.region_3.4_spmd, body=%wide.region_2.3_spmd.sunk | while | flops 5 | bytes 107 | solution.py:20
  69.8 5.1 gather_fusion
  75.1 3.6 fusion.21
  78.7 3.3 fusion.23
  82.0 68.7 %all-gather.4.cloned.1.call-done = bf16[2048,5248]{1,0:T(8,128)(2,1)} async-done(((bf16[128,5248]{1,0:T(8,128)(2,1)}), bf16[2048,5248]{1,0:T(8,128)(2,1)}) %all-gather.4.cloned.1.call-update) | async-done | bytes 21495824 | tf_op jit(solution)/shard_map/all_gather | solution.py:140
  152.9 3.0 copy.104
  155.8 6.2 %fusion.62 = f32[1024,3,256]{2,0,1:T(8,128)S(1)} fusion(bf16[1024,2048,1]{1,0,2:T(8,128)(2,1)} %bitcast.193, bf16[3,256,2048]{2,1,0:T(8,128)(2,1)} %bitcast.197), kind=kOutput, calls=%fused_computation.127 | convolution fusion | flops 3221225472 | bytes 10485760 | tf_op jit(solution)/shard_map/dot_general | solution.py:161
  168.6 3.3 divide_multiply_fusion
  171.9 2.8 reshape_squeeze.3
  177.1 95.7 %while.43 = (s32[]{:T(128)}, f32[2,128,128]{2,1,0:T(8,128)S(1)}, s32[]{:T(128)}, f32[8,128,2,128]{1,0,3,2:T(8,128)}, s32[8,128]{1,0:T(8,128)S(1)}, /*index=5*/f3...) while((s32[]{:T(128)}, f32[2,128,128]{2,1,0:T(8,128)S(1)}, ...), condition=%wide.region_11.12_spmd.clone, body=%wide.region_9.11_spmd.clone.sunk | while | flops 205996416 | bytes 3712938 | solution.py:82
  182.7 4.8 dynamic_update_slice.6
  194.7 4.8 dynamic_update_slice.6
  206.6 4.8 dynamic_update_slice.6
  218.6 4.8 dynamic_update_slice.6
  230.6 4.8 dynamic_update_slice.6
  242.5 4.8 dynamic_update_slice.6
  254.5 4.8 dynamic_update_slice.6
  266.5 4.8 dynamic_update_slice.6
  282.2 18.9 %all_gather.22 = bf16[16,2,128]{2,1,0:T(2,128)(2,1)S(1)} all-gather(bf16[1,2,128]{2,1,0:T(2,128)(2,1)S(1)} %fusion.52), channel_id=1, replica_groups=mesh['ctx'=16,'mp'=4,'rep'=2] {'ctx'}, dimensions={0}, use_global_device_ids=true | all-gather | bytes 8704 | tf_op jit(solution)/shard_map/all_gather | solution.py:26
  301.1 6.1 %all-gather.6.cloned.1.call-done = bf16[32,128,128]{2,1,0:T(8,128)(2,1)} async-done(((bf16[2,128,128]{2,1,0:T(8,128)(2,1)}), bf16[32,128,128]{2,1,0:T(8,128)(2,1)}) %all-gather.6.cloned.1.call-update) | async-done | bytes 1048592 | tf_op jit(solution)/shard_map/all_gather | solution.py:26
  307.2 16.2 %while.44 = (s32[]{:T(128)}, f32[2,128,128]{2,1,0:T(8,128)S(1)}, s32[]{:T(128)}, bf16[16,2,128]{2,1,0:T(2,128)(2,1)S(1)}, bf16[16,2,128,128]{3,2,1,0:T(8,128)(2,1)}, /*index=5*/s32[]{:T(128)}, s32[]{:T(128)}) while((s32[]{:T(128)}, f32[2,128,128]{2,1,0:T(8,128)S(1)}, s32[]{:T(128)}, bf16[16,2,128]{2,1,0:T(2,128)(2,1)S(1)}, ...), condition=%wide.region_14.15_spmd.clone, body=%wide.region_13.14_spmd.clone.sunk | while | flops 164100 | bytes 330345 | solution.py:43
  323.4 2.9 multiply_reduce_fusion.1
  326.4 4.5 convolution_convert_fusion
  331.2 14.2 %slice.81 = bf16[2048,4224]{1,0:T(8,128)(2,1)} slice(bf16[2048,5248]{1,0:T(8,128)(2,1)} %all-gather.4.cloned.1.call-done), slice={[0:2048], [1024:5248]} | slice | bytes 34603008 | tf_op jit(solution)/shard_map/slice | solution.py:143
  345.4 22.6 %copy.114 = bf16[2048,4224]{0,1:T(8,128)(2,1)} copy(bf16[2048,4224]{1,0:T(8,128)(2,1)} %slice.81) | data formatting | bytes 34603008 | tf_op jit(solution)/shard_map/slice | solution.py:143
  368.0 147.3 %all-reduce.3.cloned.1.call-done = bf16[1024,2048]{1,0:T(8,128)(2,1)} async-done(((bf16[1024,2048]{1,0:T(8,128)(2,1)}), bf16[1024,2048]{1,0:T(8,128)(2,1)}) %all-reduce.3.cloned.1.call-update) | async-done | bytes 4194320 | tf_op jit(solution)/shard_map/psum | solution.py:205
  515.3 3.2 multiply_reduce_fusion
  518.5 11.2 %fusion.19 = f32[512,2,1408]{2,0,1:T(8,128)S(1)} fusion(bf16[2048,3,1408]{0,2,1:T(8,128)(2,1)} %bitcast.190, f32[512,2048]{1,0:T(8,128)S(1)} %get-tuple-element.362, f32[2048]{0:T(1024)S(1)} %copy-done.9, f32[512]{0:T(512)S(1)} %add_rsqrt_fusion.2), kind=kOutput, calls=%fused_computation.36 | convolution fusion | flops 5908725760 | bytes 21506048 | tf_op jit(solution)/shard_map/td,dcf->tcf/dot_general | solution.py:210
  529.7 7.3 %fusion.25 = bf16[512,2048]{1,0:T(8,128)(2,1)} fusion(bf16[2048,3,1408]{0,2,1:T(8,128)(2,1)} %bitcast.191, f32[512,2,1408]{2,0,1:T(8,128)S(1)} %fusion.19), kind=kOutput, calls=%fused_computation.51 | convolution fusion | flops 2958163968 | bytes 13631488 | tf_op jit(solution)/shard_map/dot_general | solution.py:214
  537.2 29.1 %reduce-scatter.2.cloned.1.call-done = bf16[512,512]{1,0:T(8,128)(2,1)} async-done(((bf16[512,2048]{1,0:T(8,128)(2,1)}), bf16[512,512]{1,0:T(8,128)(2,1)}) %reduce-scatter.2.cloned.1.call-update) | async-done | bytes 524304 | tf_op jit(solution)/shard_map/reduce_scatter | solution.py:217
  (255 shorter events, 103.8 us)
Async XLA Ops:
  6.5 3.1 copy-start.3
  6.5 144.2 %all-gather.4.cloned.1.call-start = ((), (), s32[]{:S(2)}) async-start(), calls=%async_computation.2 | async-start | bytes 22839296 | tf_op jit(solution)/shard_map/all_gather | solution.py:140
  11.1 23.5 %copy-start.6 = (s32[8]{0:T(128)S(1)}, s32[8]{0:T(128)}, u32[]{:S(2)}) copy-start(s32[8]{0:T(128)} %param.19) | copy-start | bytes 100
  11.1 23.5 %copy-start.8 = (s32[8]{0:T(128)S(1)}, s32[8]{0:T(128)}, u32[]{:S(2)}) copy-start(s32[8]{0:T(128)} %param.18) | copy-start | bytes 100
  11.2 24.3 %copy-start.7 = (s32[32]{0:T(128)S(1)}, s32[32]{0:T(128)}, u32[]{:S(2)}) copy-start(s32[32]{0:T(128)} %param.20) | copy-start | bytes 388
  11.2 24.6 %copy-start.10 = (u32[128]{0:T(128)S(1)}, u32[128]{0:T(128)}, u32[]{:S(2)}) copy-start(u32[128]{0:T(128)} %constant.161) | copy-start | bytes 1540
  34.5 272.6 %all-gather.6.cloned.1.call-start = ((), (), s32[]{:S(2)}) async-start(), calls=%async_computation.5 | async-start | bytes 1114112 | tf_op jit(solution)/shard_map/all_gather | solution.py:26
  69.8 5.2 copy-start.4
  74.9 3.8 copy-start
  74.9 3.8 copy-start.5
  162.1 1.7 copy-start.2
  273.5 241.7 %all-reduce.3.cloned.1.call-start = ((), (), s32[]{:S(2)}) async-start(), calls=%async_computation.3 | async-start | bytes 8388608 | tf_op jit(solution)/shard_map/psum | solution.py:205
  331.0 235.3 %reduce-scatter.2.cloned.1.call-start = ((), (), s32[]{:S(2)}) async-start(), calls=%async_computation.4 | async-start | bytes 2621440 | tf_op jit(solution)/shard_map/reduce_scatter | solution.py:217
  515.3 3.2 copy-start.9
  518.5 11.2 %copy-start.1 = (f32[512,2048]{1,0:T(8,128)}, f32[512,2048]{1,0:T(8,128)S(1)}, u32[]{:S(2)}) copy-start(f32[512,2048]{1,0:T(8,128)S(1)} %get-tuple-element.362) | copy-start | bytes 12582916
Sparse Core Ops, SparseCore 0:
  34.7 116.0 all-gather.3
  273.7 33.4 all-gather.5
  331.1 184.1 all-reduce.2
  537.2 29.0 reduce-scatter.1
where the time goes:
time: 578 us; the launch traced here: 575 us
  waiting for transfers between devices  251 us (43%)
  local copies, waits for them, and re-layouts  127 us (22%)
  other arithmetic  65.4 us (11%)
  blocking collectives  54 us (9%)
  matrix products  42.7 us (7%)
  loops' own time  20.7 us (4%)
  between operations  14.2 us (2%)
    psum x1, waiting for transfers between devices, shards(): lax.psum(attn_term.astype(jnp.bfloat16), ('mp', 'rep')).astype(jnp.float32)  147 us
    all_gather x1, waiting for transfers between devices, shards(): served = lax.all_gather(arrived, 'ctx', axis=0, tiled=True)  68.7 us
    dynamic_update_slice x16, local copies, waits for them, and re-layouts, block_recurrence(): lax.scan(advance, (state_init, count_init), (queries, keys_in, values_in,...  38.8 us
    slice x2, local copies, waits for them, and re-layouts, shards(): served[:, 4 * head_cols:].reshape(model_width, 3, hidden_block)  36.8 us
    reduce_scatter x1, waiting for transfers between devices, shards(): lax.psum_scatter(down_term.astype(jnp.bfloat16), 'mp', scatter_dimension=...  29.1 us
    all_to_all x1, blocking collectives, shards(): lax.all_to_all(packed, 'mp', split_axis=1, concat_axis=0, tiled=True)  22 us
    all_gather x1, blocking collectives, entering_2(): lax.all_gather(part.astype(kind), axis)  18.9 us
    select_n x16, other arithmetic, entering_step(): return jax.tree.map(lambda a, b: jnp.where(reached, a, b), new, before)  15.5 us
  transfers between devices with their start and end apart: 4, of which 4 were waited for; matrix products, arithmetic and copies ran while one was open for 12% of the time, Pallas kernels for 0%

commit v1 on v0

--- a/solution.py
+++ b/solution.py
@@ -135,7 +135,10 @@
     gate_up = jnp.transpose(gate_up, (1, 2, 0, 3)).reshape(width_local, mp_count, 2 * hidden_block)
     down_rows = jnp.transpose(down_rows, (2, 0, 1))
     packed = jnp.concatenate([mixer_in, mixer_out, gate_up, down_rows], axis=2).astype(jnp.bfloat16)
-    arrived = lax.all_to_all(packed, "mp", split_axis=1, concat_axis=0, tiled=True)
+    arrived = jnp.concatenate(
+        lax.all_to_all(jnp.stack(jnp.split(packed, lax.axis_size("mp"), axis=1)), "mp", 0, 0),
+        axis=0,
+    )
     arrived = arrived.reshape(mp_count * width_local, packed.shape[2])
     served = lax.all_gather(arrived, "ctx", axis=0, tiled=True)
     w_mixer = served[:, : 3 * head_cols]

time: 578 us -> 579 us (level)
  no operation moved by 1% of the time
where the time goes in v1:
time: 579 us; the launch traced here: 575 us
  waiting for transfers between devices  253 us (44%)
  local copies, waits for them, and re-layouts  125 us (22%)
  other arithmetic  65.6 us (11%)
  blocking collectives  54 us (9%)
  matrix products  42.7 us (7%)
  loops' own time  20.7 us (4%)
  between operations  14.2 us (2%)
    psum x1, waiting for transfers between devices, shards(): lax.psum(attn_term.astype(jnp.bfloat16), ('mp', 'rep')).astype(jnp.float32)  147 us
    all_gather x1, waiting for transfers between devices, shards(): served = lax.all_gather(arrived, 'ctx', axis=0, tiled=True)  68.7 us
    dynamic_update_slice x16, local copies, waits for them, and re-layouts, block_recurrence(): lax.scan(advance, (state_init, count_init), (queries, keys_in, values_in,...  38.8 us
    slice x2, local copies, waits for them, and re-layouts, shards(): served[:, 4 * head_cols:].reshape(model_width, 3, hidden_block)  36.8 us
    reduce_scatter x1, waiting for transfers between devices, shards(): lax.psum_scatter(down_term.astype(jnp.bfloat16), 'mp', scatter_dimension=...  29.1 us
    all_to_all x1, blocking collectives, shards(): lax.all_to_all(jnp.stack(jnp.split(packed, lax.axis_size('mp'), axis=1)),...  22 us
    all_gather x1, blocking collectives, entering_2(): lax.all_gather(part.astype(kind), axis)  19 us
    select_n x16, other arithmetic, entering_step(): return jax.tree.map(lambda a, b: jnp.where(reached, a, b), new, before)  15.5 us
  transfers between devices with their start and end apart: 4, of which 4 were waited for; matrix products, arithmetic and copies ran while one was open for 12% of the time, Pallas kernels for 0%

profile of v1, /device:TPU:1, one launch (start us, length us, event | category | flops | bytes accessed | tf_op | source)
XLA Modules:
  0.0 575.5 jit_solution(7016973023435856332)
XLA Ops:
  12.8 22.0 %all_to_all.5 = bf16[4,32,1,5248]{3,1,2,0:T(8,128)(2,1)} all-to-all(bf16[4,32,1,5248]{3,1,2,0:T(8,128)(2,1)S(1)} %pad_maximum_fusion.1), channel_id=1, replica_groups=mesh['ctx'=16,'mp'=4,'rep'=2] {'mp'}, dimensions={0} | all-to-all | bytes 2686976 | tf_op jit(solution)/shard_map/all_to_all | solution.py:139
  37.9 13.0 %all-reduce = s32[16]{0:T(128)S(1)} all-reduce(s32[16]{0:T(128)S(1)} %dynamic-update-slice), channel_id=1, replica_groups=mesh['ctx'=16,'mp'=4,'rep'=2] {'ctx'}, use_global_device_ids=true, to_apply=%add | all-reduce | flops 16 | bytes 128
  51.0 18.5 %while.42 = (s32[]{:T(128)}, s32[]{:T(128)}, s32[]{:T(128)}, s32[16]{0:T(128)S(1)}, s32[]{:T(128)}) while((s32[]{:T(128)}, s32[]{:T(128)}, s32[]{:T(128)}, s32[16]{0:T(128)S(1)}, s32[]{:T(128)}) %tuple.99), condition=%wide.region_3.4_spmd, body=%wide.region_2.3_spmd.sunk | while | flops 5 | bytes 107 | solution.py:20
  70.1 5.1 gather_fusion
  75.4 3.6 fusion.21
  79.0 3.3 fusion.23
  82.3 68.7 %all-gather.4.cloned.1.call-done = bf16[2048,5248]{1,0:T(8,128)(2,1)} async-done(((bf16[128,5248]{1,0:T(8,128)(2,1)}), bf16[2048,5248]{1,0:T(8,128)(2,1)}) %all-gather.4.cloned.1.call-update) | async-done | bytes 21495824 | tf_op jit(solution)/shard_map/all_gather | solution.py:143
  153.2 3.0 copy.107
  156.1 6.2 %fusion.62 = f32[1024,3,256]{2,0,1:T(8,128)S(1)} fusion(bf16[1024,2048,1]{1,0,2:T(8,128)(2,1)} %bitcast.197, bf16[3,256,2048]{2,1,0:T(8,128)(2,1)} %bitcast.201), kind=kOutput, calls=%fused_computation.132 | convolution fusion | flops 3221225472 | bytes 10485760 | tf_op jit(solution)/shard_map/dot_general | solution.py:164
  168.9 3.3 divide_multiply_fusion
  172.2 2.8 reshape_squeeze.3
  177.4 95.7 %while.43 = (s32[]{:T(128)}, f32[2,128,128]{2,1,0:T(8,128)S(1)}, s32[]{:T(128)}, f32[8,128,2,128]{1,0,3,2:T(8,128)}, s32[8,128]{1,0:T(8,128)S(1)}, /*index=5*/f3...) while((s32[]{:T(128)}, f32[2,128,128]{2,1,0:T(8,128)S(1)}, ...), condition=%wide.region_11.12_spmd.clone, body=%wide.region_9.11_spmd.clone.sunk | while | flops 205996416 | bytes 3712938 | solution.py:82
  183.0 4.8 dynamic_update_slice.6
  195.0 4.8 dynamic_update_slice.6
  206.9 4.8 dynamic_update_slice.6
  218.9 4.8 dynamic_update_slice.6
  230.9 4.8 dynamic_update_slice.6
  242.8 4.8 dynamic_update_slice.6
  254.8 4.8 dynamic_update_slice.6
  266.8 4.8 dynamic_update_slice.6
  281.2 19.0 %all_gather.22 = bf16[16,2,128]{2,1,0:T(2,128)(2,1)S(1)} all-gather(bf16[1,2,128]{2,1,0:T(2,128)(2,1)S(1)} %fusion.52), channel_id=1, replica_groups=mesh['ctx'=16,'mp'=4,'rep'=2] {'ctx'}, dimensions={0}, use_global_device_ids=true | all-gather | bytes 8704 | tf_op jit(solution)/shard_map/all_gather | solution.py:26
  300.2 7.3 %all-gather.6.cloned.1.call-done = bf16[32,128,128]{2,1,0:T(8,128)(2,1)} async-done(((bf16[2,128,128]{2,1,0:T(8,128)(2,1)}), bf16[32,128,128]{2,1,0:T(8,128)(2,1)}) %all-gather.6.cloned.1.call-update) | async-done | bytes 1048592 | tf_op jit(solution)/shard_map/all_gather | solution.py:26
  307.5 16.2 %while.44 = (s32[]{:T(128)}, f32[2,128,128]{2,1,0:T(8,128)S(1)}, s32[]{:T(128)}, bf16[16,2,128]{2,1,0:T(2,128)(2,1)S(1)}, bf16[16,2,128,128]{3,2,1,0:T(8,128)(2,1)}, /*index=5*/s32[]{:T(128)}, s32[]{:T(128)}) while((s32[]{:T(128)}, f32[2,128,128]{2,1,0:T(8,128)S(1)}, s32[]{:T(128)}, bf16[16,2,128]{2,1,0:T(2,128)(2,1)S(1)}, ...), condition=%wide.region_14.15_spmd.clone, body=%wide.region_13.14_spmd.clone.sunk | while | flops 164100 | bytes 330345 | solution.py:43
  323.7 2.9 multiply_reduce_fusion.1
  326.8 4.5 convolution_convert_fusion
  331.5 14.2 %slice.81 = bf16[2048,4224]{1,0:T(8,128)(2,1)} slice(bf16[2048,5248]{1,0:T(8,128)(2,1)} %all-gather.4.cloned.1.call-done), slice={[0:2048], [1024:5248]} | slice | bytes 34603008 | tf_op jit(solution)/shard_map/slice | solution.py:146
  345.7 22.6 %copy.117 = bf16[2048,4224]{0,1:T(8,128)(2,1)} copy(bf16[2048,4224]{1,0:T(8,128)(2,1)} %slice.81) | data formatting | bytes 34603008 | tf_op jit(solution)/shard_map/slice | solution.py:146
  368.3 147.3 %all-reduce.3.cloned.1.call-done = bf16[1024,2048]{1,0:T(8,128)(2,1)} async-done(((bf16[1024,2048]{1,0:T(8,128)(2,1)}), bf16[1024,2048]{1,0:T(8,128)(2,1)}) %all-reduce.3.cloned.1.call-update) | async-done | bytes 4194320 | tf_op jit(solution)/shard_map/psum | solution.py:208
  515.6 3.2 multiply_reduce_fusion
  518.9 11.2 %fusion.19 = f32[512,2,1408]{2,0,1:T(8,128)S(1)} fusion(bf16[2048,3,1408]{0,2,1:T(8,128)(2,1)} %bitcast.194, f32[512,2048]{1,0:T(8,128)S(1)} %get-tuple-element.362, f32[2048]{0:T(1024)S(1)} %copy-done.10, f32[512]{0:T(512)S(1)} %add_rsqrt_fusion.2), kind=kOutput, calls=%fused_computation.36 | convolution fusion | flops 5908725760 | bytes 21506048 | tf_op jit(solution)/shard_map/td,dcf->tcf/dot_general | solution.py:213
  530.1 7.3 %fusion.25 = bf16[512,2048]{1,0:T(8,128)(2,1)} fusion(bf16[2048,3,1408]{0,2,1:T(8,128)(2,1)} %bitcast.195, f32[512,2,1408]{2,0,1:T(8,128)S(1)} %fusion.19), kind=kOutput, calls=%fused_computation.51 | convolution fusion | flops 2958163968 | bytes 13631488 | tf_op jit(solution)/shard_map/dot_general | solution.py:217
  537.5 29.1 %reduce-scatter.2.cloned.1.call-done = bf16[512,512]{1,0:T(8,128)(2,1)} async-done(((bf16[512,2048]{1,0:T(8,128)(2,1)}), bf16[512,512]{1,0:T(8,128)(2,1)}) %reduce-scatter.2.cloned.1.call-update) | async-done | bytes 524304 | tf_op jit(solution)/shard_map/reduce_scatter | solution.py:220
  (259 shorter events, 102.8 us)
Async XLA Ops:
  6.5 3.1 copy-start.3
  6.5 144.5 %all-gather.4.cloned.1.call-start = ((), (), s32[]{:S(2)}) async-start(), calls=%async_computation.2 | async-start | bytes 22839296 | tf_op jit(solution)/shard_map/all_gather | solution.py:143
  12.4 22.5 %copy-start.7 = (s32[8]{0:T(128)S(1)}, s32[8]{0:T(128)}, u32[]{:S(2)}) copy-start(s32[8]{0:T(128)} %param.19) | copy-start | bytes 100
  12.4 22.5 %copy-start.9 = (s32[8]{0:T(128)S(1)}, s32[8]{0:T(128)}, u32[]{:S(2)}) copy-start(s32[8]{0:T(128)} %param.18) | copy-start | bytes 100
  12.4 23.3 %copy-start.8 = (s32[32]{0:T(128)S(1)}, s32[32]{0:T(128)}, u32[]{:S(2)}) copy-start(s32[32]{0:T(128)} %param.20) | copy-start | bytes 388
  12.5 23.6 %copy-start.11 = (u32[128]{0:T(128)S(1)}, u32[128]{0:T(128)}, u32[]{:S(2)}) copy-start(u32[128]{0:T(128)} %constant.161) | copy-start | bytes 1540
  34.8 272.7 %all-gather.6.cloned.1.call-start = ((), (), s32[]{:S(2)}) async-start(), calls=%async_computation.5 | async-start | bytes 1114112 | tf_op jit(solution)/shard_map/all_gather | solution.py:26
  70.1 5.2 copy-start.5
  75.2 3.8 copy-start
  75.2 3.8 copy-start.6
  162.4 1.7 copy-start.2
  273.8 241.8 %all-reduce.3.cloned.1.call-start = ((), (), s32[]{:S(2)}) async-start(), calls=%async_computation.3 | async-start | bytes 8388608 | tf_op jit(solution)/shard_map/psum | solution.py:208
  278.4 2.6 copy-start.4
  331.3 235.3 %reduce-scatter.2.cloned.1.call-start = ((), (), s32[]{:S(2)}) async-start(), calls=%async_computation.4 | async-start | bytes 2621440 | tf_op jit(solution)/shard_map/reduce_scatter | solution.py:220
  515.6 3.2 copy-start.10
  518.9 11.2 %copy-start.1 = (f32[512,2048]{1,0:T(8,128)}, f32[512,2048]{1,0:T(8,128)S(1)}, u32[]{:S(2)}) copy-start(f32[512,2048]{1,0:T(8,128)S(1)} %get-tuple-element.362) | copy-start | bytes 12582916
Sparse Core Ops, SparseCore 0:
  35.0 116.0 all-gather.3
  274.0 33.5 all-gather.5
  331.4 184.1 all-reduce.2
  537.6 29.0 reduce-scatter.1
